TPU v7x, 32 devices: a whole 2x2x4 slice. The times are simulated.
32 devices in a mesh: groups: 2 (over y), rows: 4 (over z), blocks: 2 (over x), cols: 2 (over core).
Axes of the slice: x: 2, y: 2, z: 4, core: 2. Of those that a mesh axis runs over, the one named last changes fastest.
Arguments:
- inputs: bfloat16 [4096, 1024], P(('groups', 'rows')), parts along dimension 0, may hold values from -6 to 6
- projection: bfloat16 [1024, 8192], P(None, ('groups', 'blocks', 'cols')), parts along dimension 1, may hold values from -0.1875 to 0.1875
- phases: bfloat16 [8192], P(('groups', 'blocks', 'cols')), parts along dimension 0, may hold values from -3.140625 to 3.140625
- inverse_blocks: float32 [4, 2048, 2048], P(('groups', 'blocks'), 'rows'), parts along dimension 0, as said below
- labels: int32 [4096], P(('groups', 'rows')), parts along dimension 0, may hold values from 0 to 999
- predictions: float32 [4096, 1000], P(('groups', 'rows'), 'cols'), parts along dimension 0, may hold values from -4 to 4
- coefficients: float32 [8192, 1000], P(('groups', 'blocks', 'rows'), 'cols'), parts along dimension 0, may hold values from -3 to 3
Outputs:
- new_coefficients: float32 [8192, 1000], P(('groups', 'blocks', 'rows'), 'cols'), parts along dimension 0
- new_predictions: float32 [4096, 1000], P(('groups', 'rows'), 'cols'), parts along dimension 0
There are 2 independent parts, one for each index of `groups`. A program takes and returns all parts, laid end to end along the dimension named above; each array names one. Nothing has to cross between parts.
Inputs may be any that keep to these rules, and one draw needn't show every extreme that they name: `inverse_blocks`: one dense preconditioner for each feature block.
All inputs are finite; a program needn't handle non-finite values.
Results may differ from a plain program's by a relative error of at most 0.0029.
Values may be sent and summed in bfloat16 or wider, within the bound.
No kernel may reach another device: no remote copies, remote signals or barrier semaphores. Data moves between devices by JAX's collectives and lax.ppermute only.
A program may use at most 64 MiB of HBM per device.

v0:
```python
import jax
import jax.numpy as jnp
from jax import lax
from jax.sharding import PartitionSpec as P

DAMPING = 0.5


def cosine_features(inputs, projection, phases):
    angles = (
        jnp.dot(inputs, projection, preferred_element_type=jnp.float32)
        + phases.astype(jnp.float32)[None, :]
    )
    return jnp.cos(angles).astype(jnp.bfloat16)


def shards(inputs, projection, phases, inverse_blocks, labels, predictions, coefficients):
    out_width = predictions.shape[1]
    classes = lax.axis_index("cols") * out_width + jnp.arange(out_width, dtype=jnp.int32)
    onehot = (labels[:, None] == classes[None, :]).astype(jnp.float32)
    residual = (onehot - predictions).astype(jnp.bfloat16)
    half_features = cosine_features(inputs, projection, phases)
    features_full = lax.all_gather(half_features, "cols", axis=1, tiled=True)
    local_inverse = inverse_blocks[0]
    column_slice = features_full
    own_gradient = lax.psum_scatter(
        lax.dot_general(
            column_slice, residual, (((0,), (0,)), ((), ())), preferred_element_type=jnp.float32
        ),
        "rows",
        scatter_dimension=0,
        tiled=True,
    )
    gradient = lax.all_gather(own_gradient, "rows", axis=0, tiled=True)
    solved = jnp.dot(local_inverse, gradient, precision=lax.Precision.HIGHEST)
    step_update = DAMPING * solved
    new_coefficients = coefficients + step_update
    column_slice = features_full
    contribution = jnp.dot(
        column_slice,
        lax.all_gather(step_update.astype(jnp.bfloat16), "rows", axis=0, tiled=True),
        preferred_element_type=jnp.float32,
    )
    summed = lax.psum(contribution, "blocks")
    return (new_coefficients, predictions + summed)


def solution(mesh):
    return jax.shard_map(
        shards,
        mesh=mesh,
        in_specs=(
            P(("groups", "rows"), None),
            P(None, ("groups", "blocks", "cols")),
            P(("groups", "blocks", "cols")),
            P(("groups", "blocks"), "rows", None),
            P(("groups", "rows")),
            P(("groups", "rows"), "cols"),
            P(("groups", "blocks", "rows"), "cols"),
        ),
        out_specs=(P(("groups", "blocks", "rows"), "cols"), P(("groups", "rows"), "cols")),
        check_vma=False,
    )
```

profile of v0, /device:TPU:0, one launch (start us, length us, event | category | flops | bytes accessed | tf_op | source)
XLA Modules:
  0.0 311.2 jit_solution(1773116370345842166)
XLA Ops:
  7.2 0.0 copy-start
  7.2 0.0 all-gather.4.cloned.1.call-start
  7.2 0.8 convert_element_type.15
  8.0 0.7 copy-done
  8.8 0.0 copy-start.1
  8.8 0.0 copy-start.2
  8.8 9.8 %cosine_convert_fusion = bf16[512,1024]{1,0:T(8,128)(2,1)} fusion(bf16[512,1024]{1,0:T(8,128)(2,1)} %param.7, bf16[1024,1024]{1,0:T(8,128)(2,1)S(1)} %copy-done, f32[1024]{0:T(1024)S(1)} %convert_element_type.15), kind=kOutput, calls=%fused_computation.2 | convolution fusion | flops 1074790400 | bytes 4198400 | tf_op jit(solution)/shard_map/dot_general | solution.py:11
  18.6 0.0 all-gather.4.cloned.1.call-update
  18.6 0.0 reduce-scatter.2.cloned.1.call-start
  18.7 13.4 %all-gather.4.cloned.1.call-done = bf16[512,2048]{1,0:T(8,128)(2,1)} async-done(((bf16[512,1024]{1,0:T(8,128)(2,1)}), bf16[512,2048]{1,0:T(8,128)(2,1)}) %all-gather.4.cloned.1.call-update) | async-done | bytes 2097168 | tf_op jit(solution)/shard_map/all_gather | solution.py:23
  32.1 0.0 copy-done.1
  32.1 0.0 copy-done.2
  32.1 5.0 %fusion.8 = f32[2048,500]{1,0:T(8,128)} fusion(bf16[512,2048]{1,0:T(8,128)(2,1)} %all-gather.4.cloned.1.call-done, f32[512,500]{0,1:T(8,128)S(1)} %copy-done.1, s32[512]{0:T(512)S(1)} %copy-done.2, s32[500]{0:T(512)S(1)} %iota_add_fusion), kind=kOutput, calls=%fused_computation.6 | convolution fusion | flops 1049600000 | bytes 7221200 | tf_op jit(solution)/shard_map/dot_general | solution.py:27
  37.0 0.0 reduce-scatter.2.cloned.1.call-update
  37.0 0.0 all-gather.6.cloned.1.call-start
  37.1 78.0 %reduce-scatter.2.cloned.1.call-done = f32[512,500]{1,0:T(8,128)} async-done(((f32[2048,500]{1,0:T(8,128)}), f32[512,500]{1,0:T(8,128)}) %reduce-scatter.2.cloned.1.call-update) | async-done | bytes 1024016 | tf_op jit(solution)/shard_map/reduce_scatter | solution.py:26
  115.1 0.0 all-gather.6.cloned.1.call-update
  115.2 0.2 all-gather.8.cloned.1.call-start
  115.4 82.7 %all-gather.6.cloned.1.call-done = f32[2048,500]{1,0:T(8,128)} async-done(((f32[512,500]{1,0:T(8,128)}), f32[2048,500]{1,0:T(8,128)}) %all-gather.6.cloned.1.call-update) | async-done | bytes 4096016 | tf_op jit(solution)/shard_map/all_gather | solution.py:34
  198.1 17.2 %fusion.11 = (bf16[512,500]{0,1:T(8,128)(2,1)}, f32[512,500]{0,1:T(8,128)}) fusion(f32[512,500]{0,1:T(8,128)} %param.13, f32[2048,500]{1,0:T(8,128)} %all-gather.6.cloned.1.call-done, f32[1,512,2048]{2,1,0:T(8,128)} %param.10), kind=kOutput, calls=%fused_computation.10 | convolution fusion | flops 6292224000 | bytes 10850304 | tf_op jit(solution)/shard_map/dot_general | solution.py:35
  215.3 0.0 all-gather.8.cloned.1.call-update
  215.3 0.0 all-reduce.2.cloned.1.call-start
  215.4 43.9 %all-gather.8.cloned.1.call-done = bf16[2048,500]{0,1:T(8,128)(2,1)} async-done(((bf16[512,500]{0,1:T(8,128)(2,1)}), bf16[2048,500]{0,1:T(8,128)(2,1)}) %all-gather.8.cloned.1.call-update) | async-done | bytes 2048016 | tf_op jit(solution)/shard_map/all_gather | solution.py:41
  259.3 4.4 %fusion.12 = f32[512,500]{0,1:T(8,128)} fusion(bf16[512,2048]{1,0:T(8,128)(2,1)} %all-gather.4.cloned.1.call-done, bf16[2048,500]{0,1:T(8,128)(2,1)} %all-gather.8.cloned.1.call-done), kind=kOutput, calls=%fused_computation.11 | convolution fusion | flops 1048576000 | bytes 5169152 | tf_op jit(solution)/shard_map/dot_general | solution.py:39
  263.7 0.0 all-reduce.2.cloned.1.call-update
  263.8 38.6 %all-reduce.2.cloned.1.call-done = f32[512,500]{0,1:T(8,128)} async-done(((f32[512,500]{0,1:T(8,128)}), f32[512,500]{0,1:T(8,128)}) %all-reduce.2.cloned.1.call-update) | async-done | bytes 1024016 | tf_op jit(solution)/shard_map/psum | solution.py:44
  302.3 2.4 add.33
  (1 shorter events, 0.0 us)
Async XLA Ops:
  7.2 1.6 copy-start
  7.2 24.9 %all-gather.4.cloned.1.call-start = ((), (), s32[]{:S(2)}) async-start(), calls=%async_computation.1 | async-start | bytes 3145728 | tf_op jit(solution)/shard_map/all_gather | solution.py:23
  8.8 23.3 %copy-start.1 = (f32[512,500]{0,1:T(8,128)S(1)}, f32[512,500]{0,1:T(8,128)}, u32[]{:S(2)}) copy-start(f32[512,500]{0,1:T(8,128)} %param.12) | copy-start | bytes 3072004
  8.8 23.3 %copy-start.2 = (s32[512]{0:T(512)S(1)}, s32[512]{0:T(512)}, u32[]{:S(2)}) copy-start(s32[512]{0:T(512)} %param.11) | copy-start | bytes 6148
  18.6 96.5 %reduce-scatter.2.cloned.1.call-start = ((), (), s32[]{:S(2)}) async-start(), calls=%async_computation.2 | async-start | bytes 5242880 | tf_op jit(solution)/shard_map/reduce_scatter | solution.py:26
  37.0 161.1 %all-gather.6.cloned.1.call-start = ((), (), s32[]{:S(2)}) async-start(), calls=%async_computation.3 | async-start | bytes 5242880 | tf_op jit(solution)/shard_map/all_gather | solution.py:34
  115.2 144.1 %all-gather.8.cloned.1.call-start = ((), (), s32[]{:S(2)}) async-start(), calls=%async_computation.4 | async-start | bytes 2580480 | tf_op jit(solution)/shard_map/all_gather | solution.py:41
  215.3 87.0 %all-reduce.2.cloned.1.call-start = ((), (), s32[]{:S(2)}) async-start(), calls=%async_computation.5 | async-start | bytes 2064384 | tf_op jit(solution)/shard_map/psum | solution.py:44
Sparse Core Ops, SparseCore 0:
  18.7 13.2 all-gather.3
  37.2 77.9 reduce-scatter.1
  116.8 81.2 all-gather.5
  215.4 43.8 all-gather.7
  263.9 38.3 all-reduce.1
where the time goes:
time: 311 us
  waiting for transfers between devices  257 us (83%)
  matrix products  36.4 us (12%)
  between operations  13.8 us (4%)
  other arithmetic  3.21 us (1%)
    all_gather x1, waiting for transfers between devices, shards(): gradient = lax.all_gather(own_gradient, 'rows', axis=0, tiled=True)  82.7 us
    reduce_scatter x1, waiting for transfers between devices, shards(): lax.psum_scatter(lax.dot_general(column_slice, residual, (((0,), (0,)), (...  78 us
    all_gather x1, waiting for transfers between devices, shards(): lax.all_gather(step_update.astype(jnp.bfloat16), 'rows', axis=0, tiled=True)  43.9 us
    psum x1, waiting for transfers between devices, shards(): summed = lax.psum(contribution, 'blocks')  38.6 us
    dot_general x1, matrix products, shards(): solved = jnp.dot(local_inverse, gradient, precision=lax.Precision.HIGHEST)  17.2 us
    all_gather x1, waiting for transfers between devices, shards(): features_full = lax.all_gather(half_features, 'cols', axis=1, tiled=True)  13.4 us
    dot_general x1, matrix products, cosine_features(): jnp.dot(inputs, projection, preferred_element_type=jnp.float32)  9.81 us
  transfers between devices with their start and end apart: 5, of which 5 were waited for; matrix products, arithmetic and copies ran while one was open for 0% of the time, Pallas kernels for 0%

commit v1 on v0

--- a/solution.py
+++ b/solution.py
@@ -4,6 +4,27 @@
 from jax.sharding import PartitionSpec as P
 
 DAMPING = 0.5
+
+
+def joined_along(parts, dim):
+    parts = jnp.moveaxis(parts, 0, dim)
+    lengths = parts.shape
+    return parts.reshape(*lengths[:dim], lengths[dim] * lengths[dim + 1], *lengths[dim + 2 :])
+
+
+def doubled(array, axis):
+    length, index = (lax.axis_size(axis), lax.axis_index(axis))
+    pieces, bit = (array[None], 1)
+    while bit < length:
+        other = lax.ppermute(pieces, axis, [(i, i ^ bit) for i in range(length)])
+        low = index & bit == 0
+        pieces = jnp.concatenate([jnp.where(low, pieces, other), jnp.where(low, other, pieces)])
+        bit *= 2
+    return pieces
+
+
+def gather_by_bits(x, axis, dim):
+    return joined_along(doubled(x, axis), dim)
 
 
 def cosine_features(inputs, projection, phases):
@@ -38,7 +59,7 @@
     column_slice = features_full
     contribution = jnp.dot(
         column_slice,
-        lax.all_gather(step_update.astype(jnp.bfloat16), "rows", axis=0, tiled=True),
+        gather_by_bits(step_update.astype(jnp.bfloat16), "rows", 0),
         preferred_element_type=jnp.float32,
     )
     summed = lax.psum(contribution, "blocks")

time: 311 us -> 330 us (1.061)
  waiting for transfers between devices: 257 us -> 269 us
  local copies, waits for them, and re-layouts: 0.74 us -> 7.43 us
  matrix products: 36.4 us -> 29.8 us
  other arithmetic: 3.21 us -> 7.51 us
    ppermute x0 -> x2, waiting for transfers between devices: none -> 58.6 us  [doubled(): other = lax.ppermute(pieces, axis, [(i, i ^ bit) for i in range(length)])]
    all_gather x1 -> x0, waiting for transfers between devices: 43.9 us -> none  [shards(): lax.all_gather(step_update.astype(jnp.bfloat16), 'rows', axis=0, tiled=True)]
    dot_general x1, matrix products: 17.2 us -> 10.6 us  [shards(): solved = jnp.dot(local_inverse, gradient, precision=lax.Precision.HIGHEST)]
    concatenate x0 -> x2, local copies, waits for them, and re-layouts: none -> 5.91 us  [doubled(): jnp.concatenate([jnp.where(low, pieces, other), jnp.where(low, other, pie...]
  transfers between devices with their start and end apart: 5 -> 6, of which waited for: 5 -> 6; matrix products, arithmetic and copies ran while one was open for 0% -> 0% of each run, Pallas kernels for 0% -> 0%
where the time goes in v1:
time: 330 us; the launch traced here: 329 us
  waiting for transfers between devices  269 us (82%)
  matrix products  29.8 us (9%)
  between operations  13.8 us (4%)
  other arithmetic  7.51 us (2%)
  local copies, waits for them, and re-layouts  7.43 us (2%)
    all_gather x1, waiting for transfers between devices, shards(): gradient = lax.all_gather(own_gradient, 'rows', axis=0, tiled=True)  81.6 us
    reduce_scatter x1, waiting for transfers between devices, shards(): lax.psum_scatter(lax.dot_general(column_slice, residual, (((0,), (0,)), (...  77 us
    ppermute x2, waiting for transfers between devices, doubled(): other = lax.ppermute(pieces, axis, [(i, i ^ bit) for i in range(length)])  58.6 us
    psum x1, waiting for transfers between devices, shards(): summed = lax.psum(contribution, 'blocks')  38.7 us
    all_gather x1, waiting for transfers between devices, shards(): features_full = lax.all_gather(half_features, 'cols', axis=1, tiled=True)  13.4 us
    dot_general x1, matrix products, shards(): solved = jnp.dot(local_inverse, gradient, precision=lax.Precision.HIGHEST)  10.6 us
    dot_general x1, matrix products, cosine_features(): jnp.dot(inputs, projection, preferred_element_type=jnp.float32)  9.83 us
  transfers between devices with their start and end apart: 6, of which 6 were waited for; matrix products, arithmetic and copies ran while one was open for 0% of the time, Pallas kernels for 0%

profile of v1, /device:TPU:0, one launch (start us, length us, event | category | flops | bytes accessed | tf_op | source)
XLA Modules:
  0.0 329.2 jit_solution(3186903916985230293)
XLA Ops:
  7.2 0.0 copy-start
  7.2 0.0 all-gather.3.cloned.1.call-start
  7.2 0.8 convert_element_type.15
  8.0 0.7 copy-done
  8.8 9.8 %cosine_convert_fusion = bf16[512,1024]{1,0:T(8,128)(2,1)} fusion(bf16[512,1024]{1,0:T(8,128)(2,1)} %param.7, bf16[1024,1024]{1,0:T(8,128)(2,1)S(1)} %copy-done, f32[1024]{0:T(1024)S(1)} %convert_element_type.15), kind=kOutput, calls=%fused_computation.2 | convolution fusion | flops 1074790400 | bytes 4198400 | tf_op jit(solution)/shard_map/dot_general | solution.py:32
  18.6 0.0 all-gather.3.cloned.1.call-update
  18.6 0.0 reduce-scatter.2.cloned.1.call-start
  18.7 13.4 %all-gather.3.cloned.1.call-done = bf16[512,2048]{1,0:T(8,128)(2,1)} async-done(((bf16[512,1024]{1,0:T(8,128)(2,1)}), bf16[512,2048]{1,0:T(8,128)(2,1)}) %all-gather.3.cloned.1.call-update) | async-done | bytes 2097168 | tf_op jit(solution)/shard_map/all_gather | solution.py:44
  32.1 0.0 copy-done.1
  32.1 4.8 %fusion.8 = f32[2048,500]{0,1:T(8,128)} fusion(bf16[512,2048]{1,0:T(8,128)(2,1)} %all-gather.3.cloned.1.call-done, f32[512,500]{0,1:T(8,128)S(1)} %copy-done.1, s32[512]{0:T(512)S(1)} %copy-done.4, s32[500]{0:T(512)S(1)} %iota_add_fusion), kind=kOutput, calls=%fused_computation.10 | convolution fusion | flops 1049600000 | bytes 7221200 | tf_op jit(solution)/shard_map/dot_general | solution.py:48
  36.9 0.0 reduce-scatter.2.cloned.1.call-update
  36.9 0.0 all-gather.5.cloned.1.call-start
  37.0 77.0 %reduce-scatter.2.cloned.1.call-done = f32[512,500]{0,1:T(8,128)} async-done(((f32[2048,500]{0,1:T(8,128)}), f32[512,500]{0,1:T(8,128)}) %reduce-scatter.2.cloned.1.call-update) | async-done | bytes 1024016 | tf_op jit(solution)/shard_map/reduce_scatter | solution.py:47
  114.0 0.0 all-gather.5.cloned.1.call-update
  114.0 0.2 all-reduce.2.cloned.1.call-start
  114.2 81.6 %all-gather.5.cloned.1.call-done = f32[2048,500]{0,1:T(8,128)} async-done(((f32[512,500]{0,1:T(8,128)}), f32[2048,500]{0,1:T(8,128)}) %all-gather.5.cloned.1.call-update) | async-done | bytes 4096016 | tf_op jit(solution)/shard_map/all_gather | solution.py:55
  195.8 10.6 %convert_bitcast_fusion = (bf16[1,512,500]{1,2,0:T(8,128)(2,1)S(1)}, f32[512,500]{0,1:T(8,128)}) fusion(f32[512,500]{0,1:T(8,128)} %param.13, f32[2048,500]{0,1:T(8,128)} %all-gather.5.cloned.1.call-done, f32[1,512,2048]{2,1,0:T(8,128)} %param.10), kind=kOutput, calls=%fused_computation.11 | convolution fusion | flops 6292224000 | bytes 10850304 | tf_op jit(solution)/shard_map/dot_general | solution.py:56
  206.4 0.0 collective-permute-start
  206.5 0.8 copy-done.3
  207.2 12.8 %collective-permute-done = bf16[1,512,500]{1,2,0:T(8,128)(2,1)} collective-permute-done((bf16[1,512,500]{1,2,0:T(8,128)(2,1)S(1)}, bf16[1,512,500]{1,2,0:T(8,128)(2,1)}, u32[]{:S(2)}, u32[]{:S(2)}) %collective-permute-start) | collective-permute-done | bytes 512032 | tf_op jit(solution)/shard_map/ppermute | solution.py:19
  220.1 1.3 broadcast_select_fusion.3
  221.3 0.1 pad_maximum_fusion.1
  221.4 1.7 copy.10
  223.2 0.9 collective-permute-start.1
  224.1 45.8 %collective-permute-done.1 = bf16[2,512,500]{1,0,2:T(2,128)(2,1)} collective-permute-done((bf16[2,512,500]{1,0,2:T(2,128)(2,1)}, bf16[2,512,500]{1,0,2:T(2,128)(2,1)}, u32[]{:S(2)}, u32[]{:S(2)}) %collective-permute-start.1) | collective-permute-done | bytes 1024032 | tf_op jit(solution)/shard_map/ppermute | solution.py:19
  269.8 1.4 broadcast_select_fusion.1
  271.3 1.5 pad_maximum_fusion
  272.8 4.2 %copy.13 = bf16[4,512,500]{2,1,0:T(8,128)(2,1)} copy(bf16[4,512,500]{1,2,0:T(8,128)(2,1)} %pad_maximum_fusion) | data formatting | bytes 4096000 | tf_op jit(solution)/shard_map/concatenate | solution.py:21
  277.0 4.5 %fusion.13 = f32[512,500]{0,1:T(8,128)} fusion(bf16[512,2048]{1,0:T(8,128)(2,1)} %all-gather.3.cloned.1.call-done, bf16[2048,500]{1,0:T(8,128)(2,1)} %bitcast.22), kind=kOutput, calls=%fused_computation.17 | convolution fusion | flops 1048576000 | bytes 5169152 | tf_op jit(solution)/shard_map/dot_general | solution.py:60
  281.5 0.0 all-reduce.2.cloned.1.call-update
  281.5 38.7 %all-reduce.2.cloned.1.call-done = f32[512,500]{0,1:T(8,128)} async-done(((f32[512,500]{0,1:T(8,128)}), f32[512,500]{0,1:T(8,128)}) %all-reduce.2.cloned.1.call-update) | async-done | bytes 1024016 | tf_op jit(solution)/shard_map/psum | solution.py:65
  320.3 2.4 add.33
  (7 shorter events, 0.0 us)
Async XLA Ops:
  7.2 1.6 copy-start
  7.2 24.9 %all-gather.3.cloned.1.call-start = ((), (), s32[]{:S(2)}) async-start(), calls=%async_computation.1 | async-start | bytes 3145728 | tf_op jit(solution)/shard_map/all_gather | solution.py:44
  8.8 23.3 %copy-start.1 = (f32[512,500]{0,1:T(8,128)S(1)}, f32[512,500]{0,1:T(8,128)}, u32[]{:S(2)}) copy-start(f32[512,500]{0,1:T(8,128)} %param.12) | copy-start | bytes 3072004
  8.8 23.3 %copy-start.4 = (s32[512]{0:T(512)S(1)}, s32[512]{0:T(512)}, u32[]{:S(2)}) copy-start(s32[512]{0:T(512)} %param.11) | copy-start | bytes 6148
  18.6 95.4 %reduce-scatter.2.cloned.1.call-start = ((), (), s32[]{:S(2)}) async-start(), calls=%async_computation.2 | async-start | bytes 5160960 | tf_op jit(solution)/shard_map/reduce_scatter | solution.py:47
  36.9 158.9 %all-gather.5.cloned.1.call-start = ((), (), s32[]{:S(2)}) async-start(), calls=%async_computation.3 | async-start | bytes 5160960 | tf_op jit(solution)/shard_map/all_gather | solution.py:55
  114.0 206.2 %all-reduce.2.cloned.1.call-start = ((), (), s32[]{:S(2)}) async-start(), calls=%async_computation.4 | async-start | bytes 2064384 | tf_op jit(solution)/shard_map/psum | solution.py:65
  206.4 0.8 copy-start.3
  206.4 13.6 %collective-permute-start = (bf16[1,512,500]{1,2,0:T(8,128)(2,1)S(1)}, bf16[1,512,500]{1,2,0:T(8,128)(2,1)}, u32[]{:S(2)}, u32[]{:S(2)}) collective-permute-start(bf16[1,512,500]{1,2,0:T(8,128)(2,1)S(1)} %get-tuple-element.6), channel_id=1, source_target_pairs={{0,4},{4,0},{8,12},{12,8},{1,5},{5,1},{9,13},{13,9},{2,6},{6,2},{1... | collective-permute-start | bytes 1536008 | tf_op jit(solution)/shard_map/ppermute | solution.py:19
  223.2 46.7 %collective-permute-start.1 = (bf16[2,512,500]{1,0,2:T(2,128)(2,1)}, bf16[2,512,500]{1,0,2:T(2,128)(2,1)}, u32[]{:S(2)}, u32[]{:S(2)}) collective-permute-start(bf16[2,512,500]{1,0,2:T(2,128)(2,1)} %copy.10), channel_id=1, source_target_pairs={{0,8},{4,12},{8,0},{12,4},{1,9},{5,13},{9,1},{13,5},{2,10},{6,14},... | collective-permute-start | bytes 3072008 | tf_op jit(solution)/shard_map/ppermute | solution.py:19
  277.0 43.3 %copy-start.2 = (f32[512,500]{0,1:T(8,128)S(1)}, f32[512,500]{0,1:T(8,128)}, u32[]{:S(2)}) copy-start(f32[512,500]{0,1:T(8,128)} %param.12) | copy-start | bytes 3072004
Sparse Core Ops, SparseCore 0:
  18.8 13.2 all-gather.2
  37.0 76.9 reduce-scatter.1
  115.7 80.1 all-gather.4
  281.6 38.5 all-reduce.1
